TPU v7x, 128 devices: a whole 4x4x4 slice. The times are simulated.
128 devices in a mesh: row: 8 (over y, core), col: 16 (over x, z).
Axes of the slice: x: 4, y: 4, z: 4, core: 2. Of those that a mesh axis runs over, the one named last changes fastest.
Arguments:
- x_feat: bfloat16 [65536, 256], P(('row', 'col')), may hold values from -6 to 6
- block_values: bfloat16 [8, 16, 128, 128, 128], P('row', 'col')
- block_rows: int32 [8, 16, 128], P('row', 'col'), may hold values from 0 to 63, as said below
- block_cols: int32 [8, 16, 128], P('row', 'col'), may hold values from 0 to 31
- weight: bfloat16 [256, 256], replicated, may hold values from -0.375 to 0.375
- bias: float32 [256], replicated, may hold values from -3 to 3
- cotangent: bfloat16 [65536, 256], P(('row', 'col')), may hold values from -6 to 6
Outputs:
- out_act: bfloat16 [65536, 256], P(('row', 'col'))
- x_grad: bfloat16 [65536, 256], P(('row', 'col'))
- weight_grad: float32 [256, 256], replicated
- bias_grad: float32 [256], replicated
Inputs may be any that keep to these rules, and one draw needn't show every extreme that they name: `block_rows`: in tile (i, j), slots g * 8 to (g + 1) * 8 - 1 hold blocks of block rows g * 4 to (g + 1) * 4 - 1 of the tile; within a tile no pair of block row and block column repeats.
All inputs are finite; a program needn't handle non-finite values.
Results may differ from a plain program's by a relative error of at most 0.025.
Values may be sent and summed in bfloat16 or wider, within the bound.
No kernel may reach another device: no remote copies, remote signals or barrier semaphores. Data moves between devices by JAX's collectives and lax.ppermute only.
A program may use at most 64 MiB of HBM per device.

v0:
```python
import math
import jax
import jax.numpy as jnp
from jax import lax
from jax.sharding import PartitionSpec as P


def shards(x_feat, block_values, block_rows, block_cols, weight, bias, cotangent):
    block_size = block_values.shape[-1]
    block_count = block_values.shape[2]
    shard_rows = x_feat.shape[0]
    feature_width = x_feat.shape[1]
    per_shard = shard_rows // block_size
    cols_count = lax.axis_size("col")
    rows_count = lax.axis_size("row")
    per_group = block_count // cols_count
    values = block_values.reshape(cols_count, per_group, block_size, block_size)
    row_ids = block_rows.reshape(cols_count, per_group)
    col_ids = block_cols.reshape(cols_count, per_group)
    select = jnp.arange(per_shard, dtype=jnp.int32)
    gathered = lax.all_gather(x_feat, "row", axis=0, tiled=True)
    panel_blocks = gathered.reshape(rows_count * per_shard, block_size, feature_width)

    def forward_group(group):
        group_values = lax.dynamic_index_in_dim(values, group, 0, keepdims=False)
        local_rows = lax.dynamic_index_in_dim(row_ids, group, 0, keepdims=False) - group * per_shard
        group_cols = lax.dynamic_index_in_dim(col_ids, group, 0, keepdims=False)
        picked = jnp.take(panel_blocks, group_cols, axis=0)
        products = jnp.einsum(
            "bij,bjf->bif", group_values, picked, preferred_element_type=jnp.float32
        )
        onehot = (local_rows[None, :] == select[:, None]).astype(jnp.float32)
        summed = jnp.einsum("pb,bif->pif", onehot, products, precision=lax.Precision.HIGHEST)
        return summed.reshape(shard_rows, feature_width)

    count = cols_count * shard_rows
    first_group = 0 // shard_rows
    group_total = count // shard_rows

    def one_group(offset):
        return forward_group(first_group + offset)

    terms = lax.map(one_group, jnp.arange(group_total, dtype=jnp.int32))
    aggregated_sum = lax.psum_scatter(
        terms.reshape(count, feature_width).astype(jnp.bfloat16),
        "col",
        scatter_dimension=0,
        tiled=True,
    )
    pre = jnp.dot(aggregated_sum, weight, preferred_element_type=jnp.float32) + bias
    sigmoid_pre = jax.nn.sigmoid(pre)
    out_act = (pre * sigmoid_pre).astype(jnp.bfloat16)
    grad_pre = (
        cotangent.astype(jnp.float32) * sigmoid_pre * (1.0 + pre * (1.0 - sigmoid_pre))
    ).astype(jnp.bfloat16)
    local_weight = lax.dot_general(
        aggregated_sum, grad_pre, (((0,), (0,)), ((), ())), preferred_element_type=jnp.float32
    )
    local_bias = jnp.sum(grad_pre.astype(jnp.float32), axis=0)
    total_weight, total_bias = lax.psum((local_weight, local_bias), ("row", "col"))
    scale = 1.0 / math.sqrt(shard_rows * rows_count * cols_count)
    grad_agg = lax.dot_general(
        grad_pre, weight, (((1,), (1,)), ((), ())), preferred_element_type=jnp.float32
    ).astype(jnp.bfloat16)

    def backward_group(carry, group, shard_grad):
        grad_blocks = shard_grad.reshape(per_shard, block_size, feature_width)
        group_values = lax.dynamic_index_in_dim(values, group, 0, keepdims=False)
        local_rows = lax.dynamic_index_in_dim(row_ids, group, 0, keepdims=False) - group * per_shard
        group_cols = lax.dynamic_index_in_dim(col_ids, group, 0, keepdims=False)
        picked = jnp.take(grad_blocks, local_rows, axis=0)
        products = jnp.einsum(
            "bij,bif->bjf", group_values, picked, preferred_element_type=jnp.float32
        )
        return carry.at[group_cols].add(products)

    zeros_panel = jnp.zeros((rows_count * per_shard, block_size, feature_width), jnp.float32)
    gathered_grad = lax.all_gather(grad_agg, "col", axis=0, tiled=True)

    def advance_whole(group, inner):
        shard_grad = lax.dynamic_slice_in_dim(gathered_grad, group * shard_rows, shard_rows, 0)
        return backward_group(inner, group, shard_grad)

    collected = lax.fori_loop(0, cols_count, advance_whole, zeros_panel)
    feature_sum = lax.psum_scatter(
        collected.reshape(rows_count * shard_rows, feature_width).astype(jnp.bfloat16),
        "row",
        scatter_dimension=0,
        tiled=True,
    )
    return (out_act, feature_sum, total_weight * scale, total_bias * scale)


def solution(mesh):
    placed = (
        P(("row", "col"), None),
        P("row", "col", None, None, None),
        P("row", "col", None),
        P("row", "col", None),
        P(),
        P(),
        P(("row", "col"), None),
    )
    return jax.shard_map(
        shards,
        mesh=mesh,
        in_specs=placed,
        out_specs=(P(("row", "col"), None), P(("row", "col"), None), P(), P()),
        check_vma=False,
    )
```

profile of v0, /device:TPU:0, one launch (start us, length us, event | category | flops | bytes accessed | tf_op | source)
XLA Modules:
  0.0 497.0 jit_solution(14785330268408700120)
XLA Ops:
  8.5 1.3 reduce.6
  9.9 1.3 reduce.7
  11.3 26.1 %all-gather.3.cloned.1.call-done = bf16[4096,256]{1,0:T(8,128)(2,1)} async-done(((bf16[512,256]{1,0:T(8,128)(2,1)}), bf16[4096,256]{1,0:T(8,128)(2,1)}) %all-gather.3.cloned.1.call-update) | async-done | bytes 2097168 | tf_op jit(solution)/shard_map/all_gather | solution.py:21
  37.4 139.2 %while.25 = (s32[]{:T(128)}, bf16[16,512,256]{2,1,0:T(8,128)(2,1)}, s32[16]{0:T(128)S(1)}, s32[16,8]{1,0:T(8,128)S(1)}, bf16[16,8,128,128]{3,2,1,0:T(8,128)(2,1)...) while((s32[]{:T(128)}, bf16[16,512,256]{2,1,0:T(8,128)(2,1)}, ...), condition=%wide.region_1.2_spmd.clone, body=%wide.region_0.1_spmd.clone.sunk | while | flops 79955064 | bytes 5247947 | solution.py:43
  40.0 2.2 gather_fusion.1
  42.2 1.3 fusion.58
  48.7 2.2 gather_fusion.1
  50.9 1.3 fusion.58
  57.3 2.2 gather_fusion.1
  59.5 1.3 fusion.58
  66.0 2.2 gather_fusion.1
  68.2 1.3 fusion.58
  74.7 2.2 gather_fusion.1
  76.9 1.3 fusion.58
  83.5 2.2 gather_fusion.1
  92.2 2.2 gather_fusion.1
  94.4 1.3 fusion.58
  100.9 2.2 gather_fusion.1
  103.1 1.3 fusion.58
  109.6 2.2 gather_fusion.1
  111.8 1.3 fusion.58
  118.3 2.2 gather_fusion.1
  120.5 1.3 fusion.58
  127.0 2.2 gather_fusion.1
  129.2 1.3 fusion.58
  135.7 2.2 gather_fusion.1
  137.9 1.3 fusion.58
  144.4 2.2 gather_fusion.1
  146.6 1.3 fusion.58
  153.1 2.2 gather_fusion.1
  155.3 1.3 fusion.58
  161.8 2.2 gather_fusion.1
  164.0 1.3 fusion.58
  170.5 2.2 gather_fusion.1
  172.7 1.3 fusion.58
  176.7 78.3 %reduce-scatter.3.cloned.1.call-done = bf16[512,256]{1,0:T(8,128)(2,1)} async-done(((bf16[8192,256]{1,0:T(8,128)(2,1)}), bf16[512,256]{1,0:T(8,128)(2,1)}) %reduce-scatter.3.cloned.1.call-update) | async-done | bytes 262160 | tf_op jit(solution)/shard_map/reduce_scatter | solution.py:44
  255.0 2.1 convert_reduce_fusion
  259.3 50.0 %all-gather.5.cloned.1.call-done = bf16[8192,256]{1,0:T(8,128)(2,1)} async-done(((bf16[512,256]{1,0:T(8,128)(2,1)}), bf16[8192,256]{1,0:T(8,128)(2,1)}) %all-gather.5.cloned.1.call-update) | async-done | bytes 4194320 | tf_op jit(solution)/shard_map/all_gather | solution.py:78
  309.2 2.5 broadcast_in_dim.47
  311.7 100.4 %while.24 = (s32[]{:T(128)}, f32[32,128,256]{2,1,0:T(8,128)}, s32[16,8]{1,0:T(8,128)S(1)}, bf16[16,8,128,128]{3,2,1,0:T(8,128)(2,1)}, s32[16,8]{1,0:T(8,128)S(1)...) while((s32[]{:T(128)}, f32[32,128,256]{2,1,0:T(8,128)}, ...), condition=%wide.region_5.6_spmd, body=%wide.region_3.5_spmd.sunk | while | flops 67634296 | bytes 6558667 | solution.py:84
  314.6 3.4 scatter_fusion
  320.9 3.3 scatter_fusion
  327.2 3.3 scatter_fusion
  333.4 3.3 scatter_fusion
  338.4 1.3 fusion.52
  339.7 3.3 scatter_fusion
  344.6 1.3 fusion.52
  345.9 3.3 scatter_fusion
  352.2 3.3 scatter_fusion
  358.5 3.3 scatter_fusion
  364.7 3.3 scatter_fusion
  371.0 3.3 scatter_fusion
  377.2 3.4 scatter_fusion
  383.5 3.4 scatter_fusion
  389.8 3.3 scatter_fusion
  394.8 1.3 fusion.52
  396.1 3.4 scatter_fusion
  402.4 3.4 scatter_fusion
  407.4 1.3 fusion.52
  408.7 3.4 scatter_fusion
  412.1 3.9 convert_element_type.34
  416.0 65.3 %psum.15 = f32[256]{0:T(256)S(1)} all-reduce(f32[256]{0:T(256)S(1)} %get-tuple-element.211), channel_id=1, replica_groups=mesh['row'=8,'col'=16] {'row','col'}, use_global_device_ids=true, to_apply=%region_9.10 | all-reduce | flops 256 | bytes 2048 | tf_op jit(solution)/shard_map/psum | solution.py:60
  481.8 1.7 broadcast_multiply_fusion
  483.5 7.0 %reduce-scatter.5.cloned.1.call-done = bf16[512,256]{1,0:T(8,128)(2,1)} async-done(((bf16[4096,256]{1,0:T(8,128)(2,1)}), bf16[512,256]{1,0:T(8,128)(2,1)}) %reduce-scatter.5.cloned.1.call-update) | async-done | bytes 262160 | tf_op jit(solution)/shard_map/reduce_scatter | solution.py:85
  (248 shorter events, 87.6 us)
Async XLA Ops:
  7.2 247.8 %copy-start = (bf16[256,256]{1,0:T(8,128)(2,1)S(1)}, bf16[256,256]{1,0:T(8,128)(2,1)}, u32[]{:S(2)}) copy-start(bf16[256,256]{1,0:T(8,128)(2,1)} %param.15) | copy-start | bytes 393220
  7.2 30.2 %all-gather.3.cloned.1.call-start = ((), (), s32[]{:S(2)}) async-start(), calls=%async_computation.2 | async-start | bytes 2359296 | tf_op jit(solution)/shard_map/all_gather | solution.py:21
  7.9 247.1 %reduce-scatter.3.cloned.1.call-start = ((), (), s32[]{:S(2)}) async-start(), calls=%async_computation.3 | async-start | bytes 4456448 | tf_op jit(solution)/shard_map/reduce_scatter | solution.py:44
  176.6 78.4 %copy-start.2 = (bf16[512,256]{1,0:T(8,128)(2,1)S(1)}, bf16[512,256]{1,0:T(8,128)(2,1)}, u32[]{:S(2)}) copy-start(bf16[512,256]{1,0:T(8,128)(2,1)} %param.17) | copy-start | bytes 786436
  176.6 78.4 %copy-start.3 = (f32[256]{0:T(256)S(1)}, f32[256]{0:T(256)}, u32[]{:S(2)}) copy-start(f32[256]{0:T(256)} %param.16) | copy-start | bytes 3076
  176.7 132.6 %all-gather.5.cloned.1.call-start = ((), (), s32[]{:S(2)}) async-start(), calls=%async_computation.4 | async-start | bytes 4456448 | tf_op jit(solution)/shard_map/all_gather | solution.py:78
  255.0 3.2 copy-start.1
  258.2 223.7 %all-reduce.2.cloned.1.call-start = ((), (), s32[]{:S(2)}) async-start(), calls=%async_computation.6 | async-start | bytes 524288 | tf_op jit(solution)/shard_map/psum | solution.py:60
  259.2 231.3 %reduce-scatter.5.cloned.1.call-start = ((), (), s32[]{:S(2)}) async-start(), calls=%async_computation.5 | async-start | bytes 2359296 | tf_op jit(solution)/shard_map/reduce_scatter | solution.py:85
Sparse Core Ops, SparseCore 0:
  9.7 27.6 all-gather.2
  176.8 78.1 reduce-scatter.2
  258.3 50.9 all-gather.4
  315.1 141.5 all-reduce.1
  459.6 30.8 reduce-scatter.4
where the time goes:
time: 500 us; the launch traced here: 497 us
  waiting for transfers between devices  162 us (32%)
  local copies, waits for them, and re-layouts  84.2 us (17%)
  blocking collectives  65.3 us (13%)
  matrix products  64.9 us (13%)
  other arithmetic  63.5 us (13%)
  loops' own time  43 us (9%)
  between operations  13.8 us (3%)
    reduce_scatter x1, waiting for transfers between devices, shards(): lax.psum_scatter(terms.reshape(count, feature_width).astype(jnp.bfloat16)...  78.3 us
    psum x1, blocking collectives, shards(): lax.psum((local_weight, local_bias), ('row', 'col'))  65.3 us
    scatter-add x16, other arithmetic, backward_group(): return carry.at[group_cols].add(products)  53.3 us
    all_gather x1, waiting for transfers between devices, shards(): gathered_grad = lax.all_gather(grad_agg, 'col', axis=0, tiled=True)  50 us
    another operation x1, loops' own time, shards(): terms = lax.map(one_group, jnp.arange(group_total, dtype=jnp.int32))  42.4 us
    gather x16, local copies, waits for them, and re-layouts, forward_group(): picked = jnp.take(panel_blocks, group_cols, axis=0)  34.7 us
    all_gather x1, waiting for transfers between devices, shards(): gathered = lax.all_gather(x_feat, 'row', axis=0, tiled=True)  26.1 us
    dot_general x16, matrix products, forward_group(): jnp.einsum('bij,bjf->bif', group_values, picked, preferred_element_type=j...  21.1 us
  transfers between devices with their start and end apart: 5, of which 4 were waited for; matrix products, arithmetic and copies ran while one was open for 23% of the time, Pallas kernels for 0%

commit v1 on v0

--- a/solution.py
+++ b/solution.py
@@ -75,7 +75,12 @@
         return carry.at[group_cols].add(products)
 
     zeros_panel = jnp.zeros((rows_count * per_shard, block_size, feature_width), jnp.float32)
-    gathered_grad = lax.all_gather(grad_agg, "col", axis=0, tiled=True)
+    ring = [grad_agg]
+    for hop in range(15):
+        ring.append(lax.ppermute(ring[-1], "col", [(dev, (dev + 1) % 16) for dev in range(16)]))
+    gathered_grad = jnp.roll(
+        jnp.concatenate(ring[::-1], axis=0), (lax.axis_index("col") + 1) * ring[0].shape[0], axis=0
+    )
 
     def advance_whole(group, inner):
         shard_grad = lax.dynamic_slice_in_dim(gathered_grad, group * shard_rows, shard_rows, 0)

time: 500 us -> 604 us (1.21)
  waiting for transfers between devices: 162 us -> 256 us
  local copies, waits for them, and re-layouts: 84.2 us -> 94.1 us
    ppermute x0 -> x15, waiting for transfers between devices: none -> 151 us  [shards(): lax.ppermute(ring[-1], 'col', [(dev, (dev + 1) % 16) for dev in range(16)])]
    all_gather x1 -> x0, waiting for transfers between devices: 50 us -> none  [shards(): gathered_grad = lax.all_gather(grad_agg, 'col', axis=0, tiled=True)]
    unnamed x9 -> x48, local copies, waits for them, and re-layouts: 0.53 us -> 8.25 us
    reduce_scatter x1, waiting for transfers between devices: 6.98 us -> 0.01 us  [shards(): lax.psum_scatter(collected.reshape(rows_count * shard_rows, feature_width...]
  transfers between devices with their start and end apart: 5 -> 19, of which waited for: 4 -> 17; matrix products, arithmetic and copies ran while one was open for 23% -> 20% of each run, Pallas kernels for 0% -> 0%
where the time goes in v1:
time: 604 us; the launch traced here: 600 us
  waiting for transfers between devices  256 us (42%)
  local copies, waits for them, and re-layouts  94.1 us (16%)
  matrix products  65.7 us (11%)
  other arithmetic  63.4 us (10%)
  blocking collectives  62.7 us (10%)
  loops' own time  43 us (7%)
  between operations  14.1 us (2%)
    ppermute x15, waiting for transfers between devices, shards(): lax.ppermute(ring[-1], 'col', [(dev, (dev + 1) % 16) for dev in range(16)])  151 us
    reduce_scatter x1, waiting for transfers between devices, shards(): lax.psum_scatter(terms.reshape(count, feature_width).astype(jnp.bfloat16)...  78.1 us
    psum x1, blocking collectives, shards(): lax.psum((local_weight, local_bias), ('row', 'col'))  62.7 us
    scatter-add x16, other arithmetic, backward_group(): return carry.at[group_cols].add(products)  53.3 us
    another operation x1, loops' own time, shards(): terms = lax.map(one_group, jnp.arange(group_total, dtype=jnp.int32))  42.4 us
    gather x16, local copies, waits for them, and re-layouts, forward_group(): picked = jnp.take(panel_blocks, group_cols, axis=0)  34.7 us
    all_gather x1, waiting for transfers between devices, shards(): gathered = lax.all_gather(x_feat, 'row', axis=0, tiled=True)  26.1 us
    dot_general x16, matrix products, forward_group(): jnp.einsum('bij,bjf->bif', group_values, picked, preferred_element_type=j...  21.1 us
  transfers between devices with their start and end apart: 19, of which 17 were waited for; matrix products, arithmetic and copies ran while one was open for 20% of the time, Pallas kernels for 0%

profile of v1, /device:TPU:0, one launch (start us, length us, event | category | flops | bytes accessed | tf_op | source)
XLA Modules:
  0.0 600.1 jit_solution(9385483194138844369)
XLA Ops:
  9.9 1.3 reduce.7
  11.3 26.1 %all-gather.2.cloned.1.call-done = bf16[4096,256]{1,0:T(8,128)(2,1)} async-done(((bf16[512,256]{1,0:T(8,128)(2,1)}), bf16[4096,256]{1,0:T(8,128)(2,1)}) %all-gather.2.cloned.1.call-update) | async-done | bytes 2097168 | tf_op jit(solution)/shard_map/all_gather | solution.py:21
  37.4 139.2 %while.25 = (s32[]{:T(128)}, bf16[16,512,256]{2,1,0:T(8,128)(2,1)}, s32[16]{0:T(128)S(1)}, s32[16,8]{1,0:T(8,128)S(1)}, bf16[16,8,128,128]{3,2,1,0:T(8,128)(2,1)...) while((s32[]{:T(128)}, bf16[16,512,256]{2,1,0:T(8,128)(2,1)}, ...), condition=%wide.region_1.2_spmd.clone, body=%wide.region_0.1_spmd.clone.sunk | while | flops 79955064 | bytes 5247947 | solution.py:43
  40.0 2.2 gather_fusion.1
  48.7 2.2 gather_fusion.1
  50.9 1.3 fusion.58
  57.4 2.2 gather_fusion.1
  66.1 2.2 gather_fusion.1
  74.8 2.2 gather_fusion.1
  83.5 2.2 gather_fusion.1
  92.2 2.2 gather_fusion.1
  94.4 1.3 fusion.58
  100.9 2.2 gather_fusion.1
  109.6 2.2 gather_fusion.1
  118.3 2.2 gather_fusion.1
  127.0 2.2 gather_fusion.1
  135.7 2.2 gather_fusion.1
  144.4 2.2 gather_fusion.1
  153.1 2.2 gather_fusion.1
  161.8 2.2 gather_fusion.1
  170.5 2.2 gather_fusion.1
  176.7 78.1 %reduce-scatter.3.cloned.1.call-done = bf16[512,256]{1,0:T(8,128)(2,1)} async-done(((bf16[8192,256]{1,0:T(8,128)(2,1)}), bf16[512,256]{1,0:T(8,128)(2,1)}) %reduce-scatter.3.cloned.1.call-update) | async-done | bytes 262160 | tf_op jit(solution)/shard_map/reduce_scatter | solution.py:44
  254.8 2.6 convert_reduce_fusion
  259.0 8.5 %collective-permute-done = bf16[512,256]{1,0:T(8,128)(2,1)S(1)} collective-permute-done((bf16[512,256]{1,0:T(8,128)(2,1)S(1)}, bf16[512,256]{1,0:T(8,128)(2,1)S(1)}, u32[]{:S(2)}, u32[]{:S(2)}) %collective-permute-start) | collective-permute-done | bytes 262176 | tf_op jit(solution)/shard_map/ppermute | solution.py:80
  267.5 9.7 %collective-permute-done.1 = bf16[512,256]{1,0:T(8,128)(2,1)S(1)} collective-permute-done((bf16[512,256]{1,0:T(8,128)(2,1)S(1)}, bf16[512,256]{1,0:T(8,128)(2,1)S(1)}, u32[]{:S(2)}, u32[]{:S(2)}) %collective-permute-start.1) | collective-permute-done | bytes 262176 | tf_op jit(solution)/shard_map/ppermute | solution.py:80
  277.2 9.7 %collective-permute-done.2 = bf16[512,256]{1,0:T(8,128)(2,1)S(1)} collective-permute-done((bf16[512,256]{1,0:T(8,128)(2,1)S(1)}, bf16[512,256]{1,0:T(8,128)(2,1)S(1)}, u32[]{:S(2)}, u32[]{:S(2)}) %collective-permute-start.2) | collective-permute-done | bytes 262176 | tf_op jit(solution)/shard_map/ppermute | solution.py:80
  286.9 10.1 %collective-permute-done.3 = bf16[512,256]{1,0:T(8,128)(2,1)S(1)} collective-permute-done((bf16[512,256]{1,0:T(8,128)(2,1)S(1)}, bf16[512,256]{1,0:T(8,128)(2,1)S(1)}, u32[]{:S(2)}, u32[]{:S(2)}) %collective-permute-start.3) | collective-permute-done | bytes 262176 | tf_op jit(solution)/shard_map/ppermute | solution.py:80
  297.0 11.3 %collective-permute-done.4 = bf16[512,256]{1,0:T(8,128)(2,1)S(1)} collective-permute-done((bf16[512,256]{1,0:T(8,128)(2,1)S(1)}, bf16[512,256]{1,0:T(8,128)(2,1)S(1)}, u32[]{:S(2)}, u32[]{:S(2)}) %collective-permute-start.4) | collective-permute-done | bytes 262176 | tf_op jit(solution)/shard_map/ppermute | solution.py:80
  308.3 12.4 %collective-permute-done.5 = bf16[512,256]{1,0:T(8,128)(2,1)S(1)} collective-permute-done((bf16[512,256]{1,0:T(8,128)(2,1)S(1)}, bf16[512,256]{1,0:T(8,128)(2,1)S(1)}, u32[]{:S(2)}, u32[]{:S(2)}) %collective-permute-start.5) | collective-permute-done | bytes 262176 | tf_op jit(solution)/shard_map/ppermute | solution.py:80
  320.7 11.6 %collective-permute-done.6 = bf16[512,256]{1,0:T(8,128)(2,1)S(1)} collective-permute-done((bf16[512,256]{1,0:T(8,128)(2,1)S(1)}, bf16[512,256]{1,0:T(8,128)(2,1)S(1)}, u32[]{:S(2)}, u32[]{:S(2)}) %collective-permute-start.6) | collective-permute-done | bytes 262176 | tf_op jit(solution)/shard_map/ppermute | solution.py:80
  332.4 10.8 %collective-permute-done.7 = bf16[512,256]{1,0:T(8,128)(2,1)S(1)} collective-permute-done((bf16[512,256]{1,0:T(8,128)(2,1)S(1)}, bf16[512,256]{1,0:T(8,128)(2,1)S(1)}, u32[]{:S(2)}, u32[]{:S(2)}) %collective-permute-start.7) | collective-permute-done | bytes 262176 | tf_op jit(solution)/shard_map/ppermute | solution.py:80
  343.2 9.9 %collective-permute-done.8 = bf16[512,256]{1,0:T(8,128)(2,1)S(1)} collective-permute-done((bf16[512,256]{1,0:T(8,128)(2,1)S(1)}, bf16[512,256]{1,0:T(8,128)(2,1)S(1)}, u32[]{:S(2)}, u32[]{:S(2)}) %collective-permute-start.8) | collective-permute-done | bytes 262176 | tf_op jit(solution)/shard_map/ppermute | solution.py:80
  353.1 9.7 %collective-permute-done.9 = bf16[512,256]{1,0:T(8,128)(2,1)S(1)} collective-permute-done((bf16[512,256]{1,0:T(8,128)(2,1)S(1)}, bf16[512,256]{1,0:T(8,128)(2,1)S(1)}, u32[]{:S(2)}, u32[]{:S(2)}) %collective-permute-start.9) | collective-permute-done | bytes 262176 | tf_op jit(solution)/shard_map/ppermute | solution.py:80
  362.8 9.7 %collective-permute-done.10 = bf16[512,256]{1,0:T(8,128)(2,1)S(1)} collective-permute-done((bf16[512,256]{1,0:T(8,128)(2,1)S(1)}, bf16[512,256]{1,0:T(8,128)(2,1)S(1)}, u32[]{:S(2)}, u32[]{:S(2)}) %collective-permute-start.10) | collective-permute-done | bytes 262176 | tf_op jit(solution)/shard_map/ppermute | solution.py:80
  372.5 9.7 %collective-permute-done.11 = bf16[512,256]{1,0:T(8,128)(2,1)S(1)} collective-permute-done((bf16[512,256]{1,0:T(8,128)(2,1)S(1)}, bf16[512,256]{1,0:T(8,128)(2,1)S(1)}, u32[]{:S(2)}, u32[]{:S(2)}) %collective-permute-start.11) | collective-permute-done | bytes 262176 | tf_op jit(solution)/shard_map/ppermute | solution.py:80
  382.9 9.8 %collective-permute-done.12 = bf16[512,256]{1,0:T(8,128)(2,1)S(1)} collective-permute-done((bf16[512,256]{1,0:T(8,128)(2,1)S(1)}, bf16[512,256]{1,0:T(8,128)(2,1)S(1)}, u32[]{:S(2)}, u32[]{:S(2)}) %collective-permute-start.12) | collective-permute-done | bytes 262176 | tf_op jit(solution)/shard_map/ppermute | solution.py:80
  393.4 9.8 %collective-permute-done.13 = bf16[512,256]{1,0:T(8,128)(2,1)} collective-permute-done((bf16[512,256]{1,0:T(8,128)(2,1)S(1)}, bf16[512,256]{1,0:T(8,128)(2,1)}, u32[]{:S(2)}, u32[]{:S(2)}) %collective-permute-start.13) | collective-permute-done | bytes 262176 | tf_op jit(solution)/shard_map/ppermute | solution.py:80
  403.2 1.9 fusion.30
  405.2 8.0 %collective-permute-done.14 = bf16[512,256]{1,0:T(8,128)(2,1)} collective-permute-done((bf16[512,256]{1,0:T(8,128)(2,1)}, bf16[512,256]{1,0:T(8,128)(2,1)}, u32[]{:S(2)}, u32[]{:S(2)}) %collective-permute-start.14) | collective-permute-done | bytes 262176 | tf_op jit(solution)/shard_map/ppermute | solution.py:80
  419.8 2.2 constant_dynamic-slice_fusion.5
  422.0 2.5 broadcast_in_dim.47
  424.5 100.3 %while.24 = (s32[]{:T(128)}, f32[32,128,256]{2,1,0:T(8,128)}, s32[16,8]{1,0:T(8,128)S(1)}, bf16[16,8,128,128]{3,2,1,0:T(8,128)(2,1)}, s32[16,8]{1,0:T(8,128)S(1)...) while((s32[]{:T(128)}, f32[32,128,256]{2,1,0:T(8,128)}, ...), condition=%wide.region_5.6_spmd, body=%wide.region_3.5_spmd.sunk | while | flops 67634296 | bytes 6558667 | solution.py:89
  427.4 3.4 scatter_fusion
  433.7 3.3 scatter_fusion
  439.9 3.3 scatter_fusion
  446.2 3.3 scatter_fusion
  452.4 3.3 scatter_fusion
  458.7 3.3 scatter_fusion
  465.0 3.4 scatter_fusion
  471.3 3.3 scatter_fusion
  476.2 1.3 fusion.52
  477.5 3.3 scatter_fusion
  483.8 3.3 scatter_fusion
  490.0 3.4 scatter_fusion
  495.0 1.3 fusion.52
  496.3 3.3 scatter_fusion
  502.6 3.3 scatter_fusion
  508.9 3.3 scatter_fusion
  513.8 1.3 fusion.52
  515.2 3.4 scatter_fusion
  521.5 3.4 scatter_fusion
  524.8 3.9 convert_element_type.34
  528.7 62.7 %psum.15 = f32[256]{0:T(256)S(1)} all-reduce(f32[256]{0:T(256)S(1)} %copy-done.5), channel_id=1, replica_groups=mesh['row'=8,'col'=16] {'row','col'}, use_global_device_ids=true, to_apply=%region_9.10 | all-reduce | flops 256 | bytes 2048 | tf_op jit(solution)/shard_map/psum | solution.py:60
  591.9 1.7 broadcast_multiply_fusion
  (316 shorter events, 114.7 us)
Async XLA Ops:
  7.2 247.6 %copy-start = (bf16[256,256]{1,0:T(8,128)(2,1)S(1)}, bf16[256,256]{1,0:T(8,128)(2,1)}, u32[]{:S(2)}) copy-start(bf16[256,256]{1,0:T(8,128)(2,1)} %param.15) | copy-start | bytes 393220
  7.2 30.2 %all-gather.2.cloned.1.call-start = ((), (), s32[]{:S(2)}) async-start(), calls=%async_computation.2 | async-start | bytes 2359296 | tf_op jit(solution)/shard_map/all_gather | solution.py:21
  7.9 246.9 %reduce-scatter.3.cloned.1.call-start = ((), (), s32[]{:S(2)}) async-start(), calls=%async_computation.3 | async-start | bytes 4456448 | tf_op jit(solution)/shard_map/reduce_scatter | solution.py:44
  37.4 217.4 %copy-start.6 = (bf16[512,256]{1,0:T(8,128)(2,1)S(1)}, bf16[512,256]{1,0:T(8,128)(2,1)}, u32[]{:S(2)}) copy-start(bf16[512,256]{1,0:T(8,128)(2,1)} %param.17) | copy-start | bytes 786436
  37.4 217.4 %copy-start.7 = (f32[256]{0:T(256)S(1)}, f32[256]{0:T(256)}, u32[]{:S(2)}) copy-start(f32[256]{0:T(256)} %param.16) | copy-start | bytes 3076
  176.7 415.3 %all-reduce.2.cloned.1.call-start = ((), (), s32[]{:S(2)}) async-start(), calls=%async_computation.5 | async-start | bytes 524288 | tf_op jit(solution)/shard_map/psum | solution.py:60
  257.7 9.8 %collective-permute-start = (bf16[512,256]{1,0:T(8,128)(2,1)S(1)}, bf16[512,256]{1,0:T(8,128)(2,1)S(1)}, u32[]{:S(2)}, u32[]{:S(2)}) collective-permute-start(bf16[512,256]{1,0:T(8,128)(2,1)S(1)} %convolution_convert_fusion), channel_id=1, source_target_pairs={{0,1},{1,2},{2,3},{3,4},{4,5},{5,6},{6,7},{7,8},{8,9},{9,10},{10,1... | collective-permute-start | bytes 786440 | tf_op jit(solution)/shard_map/ppermute | solution.py:80
  267.5 9.7 %collective-permute-start.1 = (bf16[512,256]{1,0:T(8,128)(2,1)S(1)}, bf16[512,256]{1,0:T(8,128)(2,1)S(1)}, u32[]{:S(2)}, u32[]{:S(2)}) collective-permute-start(bf16[512,256]{1,0:T(8,128)(2,1)S(1)} %collective-permute-done), channel_id=1, source_target_pairs={{0,1},{1,2},{2,3},{3,4},{4,5},{5,6},{6,7},{7,8},{8,9},{9,10},{10,1... | collective-permute-start | bytes 786440 | tf_op jit(solution)/shard_map/ppermute | solution.py:80
  277.2 9.7 %collective-permute-start.2 = (bf16[512,256]{1,0:T(8,128)(2,1)S(1)}, bf16[512,256]{1,0:T(8,128)(2,1)S(1)}, u32[]{:S(2)}, u32[]{:S(2)}) collective-permute-start(bf16[512,256]{1,0:T(8,128)(2,1)S(1)} %collective-permute-done.1), channel_id=1, source_target_pairs={{0,1},{1,2},{2,3},{3,4},{4,5},{5,6},{6,7},{7,8},{8,9},{9,10},{10,1... | collective-permute-start | bytes 786440 | tf_op jit(solution)/shard_map/ppermute | solution.py:80
  286.9 10.1 %collective-permute-start.3 = (bf16[512,256]{1,0:T(8,128)(2,1)S(1)}, bf16[512,256]{1,0:T(8,128)(2,1)S(1)}, u32[]{:S(2)}, u32[]{:S(2)}) collective-permute-start(bf16[512,256]{1,0:T(8,128)(2,1)S(1)} %collective-permute-done.2), channel_id=1, source_target_pairs={{0,1},{1,2},{2,3},{3,4},{4,5},{5,6},{6,7},{7,8},{8,9},{9,10},{10,1... | collective-permute-start | bytes 786440 | tf_op jit(solution)/shard_map/ppermute | solution.py:80
  297.0 11.3 %collective-permute-start.4 = (bf16[512,256]{1,0:T(8,128)(2,1)S(1)}, bf16[512,256]{1,0:T(8,128)(2,1)S(1)}, u32[]{:S(2)}, u32[]{:S(2)}) collective-permute-start(bf16[512,256]{1,0:T(8,128)(2,1)S(1)} %collective-permute-done.3), channel_id=1, source_target_pairs={{0,1},{1,2},{2,3},{3,4},{4,5},{5,6},{6,7},{7,8},{8,9},{9,10},{10,1... | collective-permute-start | bytes 786440 | tf_op jit(solution)/shard_map/ppermute | solution.py:80
  308.3 12.4 %collective-permute-start.5 = (bf16[512,256]{1,0:T(8,128)(2,1)S(1)}, bf16[512,256]{1,0:T(8,128)(2,1)S(1)}, u32[]{:S(2)}, u32[]{:S(2)}) collective-permute-start(bf16[512,256]{1,0:T(8,128)(2,1)S(1)} %collective-permute-done.4), channel_id=1, source_target_pairs={{0,1},{1,2},{2,3},{3,4},{4,5},{5,6},{6,7},{7,8},{8,9},{9,10},{10,1... | collective-permute-start | bytes 786440 | tf_op jit(solution)/shard_map/ppermute | solution.py:80
  320.7 11.6 %collective-permute-start.6 = (bf16[512,256]{1,0:T(8,128)(2,1)S(1)}, bf16[512,256]{1,0:T(8,128)(2,1)S(1)}, u32[]{:S(2)}, u32[]{:S(2)}) collective-permute-start(bf16[512,256]{1,0:T(8,128)(2,1)S(1)} %collective-permute-done.5), channel_id=1, source_target_pairs={{0,1},{1,2},{2,3},{3,4},{4,5},{5,6},{6,7},{7,8},{8,9},{9,10},{10,1... | collective-permute-start | bytes 786440 | tf_op jit(solution)/shard_map/ppermute | solution.py:80
  332.4 10.8 %collective-permute-start.7 = (bf16[512,256]{1,0:T(8,128)(2,1)S(1)}, bf16[512,256]{1,0:T(8,128)(2,1)S(1)}, u32[]{:S(2)}, u32[]{:S(2)}) collective-permute-start(bf16[512,256]{1,0:T(8,128)(2,1)S(1)} %collective-permute-done.6), channel_id=1, source_target_pairs={{0,1},{1,2},{2,3},{3,4},{4,5},{5,6},{6,7},{7,8},{8,9},{9,10},{10,1... | collective-permute-start | bytes 786440 | tf_op jit(solution)/shard_map/ppermute | solution.py:80
  343.2 9.9 %collective-permute-start.8 = (bf16[512,256]{1,0:T(8,128)(2,1)S(1)}, bf16[512,256]{1,0:T(8,128)(2,1)S(1)}, u32[]{:S(2)}, u32[]{:S(2)}) collective-permute-start(bf16[512,256]{1,0:T(8,128)(2,1)S(1)} %collective-permute-done.7), channel_id=1, source_target_pairs={{0,1},{1,2},{2,3},{3,4},{4,5},{5,6},{6,7},{7,8},{8,9},{9,10},{10,1... | collective-permute-start | bytes 786440 | tf_op jit(solution)/shard_map/ppermute | solution.py:80
  353.1 9.7 %collective-permute-start.9 = (bf16[512,256]{1,0:T(8,128)(2,1)S(1)}, bf16[512,256]{1,0:T(8,128)(2,1)S(1)}, u32[]{:S(2)}, u32[]{:S(2)}) collective-permute-start(bf16[512,256]{1,0:T(8,128)(2,1)S(1)} %collective-permute-done.8), channel_id=1, source_target_pairs={{0,1},{1,2},{2,3},{3,4},{4,5},{5,6},{6,7},{7,8},{8,9},{9,10},{10,1... | collective-permute-start | bytes 786440 | tf_op jit(solution)/shard_map/ppermute | solution.py:80
  362.8 9.7 %collective-permute-start.10 = (bf16[512,256]{1,0:T(8,128)(2,1)S(1)}, bf16[512,256]{1,0:T(8,128)(2,1)S(1)}, u32[]{:S(2)}, u32[]{:S(2)}) collective-permute-start(bf16[512,256]{1,0:T(8,128)(2,1)S(1)} %collective-permute-done.9), channel_id=1, source_target_pairs={{0,1},{1,2},{2,3},{3,4},{4,5},{5,6},{6,7},{7,8},{8,9},{9,10},{10,1... | collective-permute-start | bytes 786440 | tf_op jit(solution)/shard_map/ppermute | solution.py:80
  372.5 9.7 %collective-permute-start.11 = (bf16[512,256]{1,0:T(8,128)(2,1)S(1)}, bf16[512,256]{1,0:T(8,128)(2,1)S(1)}, u32[]{:S(2)}, u32[]{:S(2)}) collective-permute-start(bf16[512,256]{1,0:T(8,128)(2,1)S(1)} %collective-permute-done.10), channel_id=1, source_target_pairs={{0,1},{1,2},{2,3},{3,4},{4,5},{5,6},{6,7},{7,8},{8,9},{9,10},{10,1... | collective-permute-start | bytes 786440 | tf_op jit(solution)/shard_map/ppermute | solution.py:80
  382.1 0.7 copy-start.1
  382.8 9.9 %collective-permute-start.12 = (bf16[512,256]{1,0:T(8,128)(2,1)S(1)}, bf16[512,256]{1,0:T(8,128)(2,1)S(1)}, u32[]{:S(2)}, u32[]{:S(2)}) collective-permute-start(bf16[512,256]{1,0:T(8,128)(2,1)S(1)} %collective-permute-done.11), channel_id=1, source_target_pairs={{0,1},{1,2},{2,3},{3,4},{4,5},{5,6},{6,7},{7,8},{8,9},{9,10},{10,1... | collective-permute-start | bytes 786440 | tf_op jit(solution)/shard_map/ppermute | solution.py:80
  392.7 0.7 copy-start.3
  393.4 9.8 %collective-permute-start.13 = (bf16[512,256]{1,0:T(8,128)(2,1)S(1)}, bf16[512,256]{1,0:T(8,128)(2,1)}, u32[]{:S(2)}, u32[]{:S(2)}) collective-permute-start(bf16[512,256]{1,0:T(8,128)(2,1)S(1)} %collective-permute-done.12), channel_id=1, source_target_pairs={{0,1},{1,2},{2,3},{3,4},{4,5},{5,6},{6,7},{7,8},{8,9},{9,10},{10,1... | collective-permute-start | bytes 786440 | tf_op jit(solution)/shard_map/ppermute | solution.py:80
  403.2 10.0 %collective-permute-start.14 = (bf16[512,256]{1,0:T(8,128)(2,1)}, bf16[512,256]{1,0:T(8,128)(2,1)}, u32[]{:S(2)}, u32[]{:S(2)}) collective-permute-start(bf16[512,256]{1,0:T(8,128)(2,1)} %collective-permute-done.13), channel_id=1, source_target_pairs={{0,1},{1,2},{2,3},{3,4},{4,5},{5,6},{6,7},{7,8},{8,9},{9,10},{10,1... | collective-permute-start | bytes 786440 | tf_op jit(solution)/shard_map/ppermute | solution.py:80
  405.1 14.3 %copy-start.2 = (bf16[512,256]{1,0:T(8,128)(2,1)S(1)}, bf16[512,256]{1,0:T(8,128)(2,1)}, u32[]{:S(2)}) copy-start(bf16[512,256]{1,0:T(8,128)(2,1)} %copy-done.1) | copy-start | bytes 786436
  405.1 188.5 %reduce-scatter.5.cloned.1.call-start = ((), (), s32[]{:S(2)}) async-start(), calls=%async_computation.4 | async-start | bytes 2359296 | tf_op jit(solution)/shard_map/reduce_scatter | solution.py:90
  405.2 14.2 %copy-start.4 = (bf16[512,256]{1,0:T(8,128)(2,1)S(1)}, bf16[512,256]{1,0:T(8,128)(2,1)}, u32[]{:S(2)}) copy-start(bf16[512,256]{1,0:T(8,128)(2,1)} %copy-done.3) | copy-start | bytes 786436
  524.8 3.9 copy-start.5
Sparse Core Ops, SparseCore 0:
  9.7 27.6 all-gather.1
  176.8 77.9 reduce-scatter.2
  405.3 142.9 all-reduce.1
  551.2 30.8 reduce-scatter.4
